TPU v7x, 512 devices: a whole 4x4x16 slice. The times are simulated.
512 devices in a mesh: sec: 2 (over z_hi), gx: 16 (over z_lo, core), gy: 16 (over x, y).
Axes of the slice: x: 4, y: 4, z: 16 (z_hi: 2, z_lo: 8; z = z_hi * 8 + z_lo), core: 2. Of those that a mesh axis runs over, the one named last changes fastest.
Arguments:
- terminal: float32 [4, 16, 256, 4096], P('sec', None, 'gx', 'gy'), may hold values from -6 to 6
- forward_temp: bfloat16 [2, 4, 16, 256, 4096], P(None, 'sec', None, 'gx', 'gy'), may hold values from -6 to 6
- conductivity: float32 [16, 256, 4096], P(None, 'gx', 'gy'), may hold values from 0.02 to 0.15
- velocity: float32 [2, 16, 256, 4096], P(None, None, 'gx', 'gy'), may hold values from -0.3 to 0.3
- fixed_mask: int32 [16, 256, 4096], P(None, 'gx', 'gy'), may hold values 0 or 1
- wells: int32 [4, 8, 3], P('sec'), may hold values from 0 to 4095, as said below
- misfit: float32 [2, 4, 8], P(None, 'sec'), may hold values from -12 to 12
- head_gradient: bfloat16 [2, 16, 256, 4096], P('sec', None, 'gx', 'gy'), may hold values from -6 to 6
- blocks: bfloat16 [32, 7, 128, 128], P('gy'), may hold values from -0.1875 to 0.1875
- block_cols: int32 [32, 7], P('gy'), may hold values from 0 to 31, as said below
Outputs:
- head_adjoint: float32 [2, 16, 256, 4096], P('sec', None, 'gx', 'gy')
- sensitivity: float32 [16, 256, 4096], P(None, 'gx', 'gy')
Inputs may be any that keep to these rules, and one draw needn't show every extreme that they name: `wells`: each row is one cell (z, x, y) with z < 16, x < 256, y < 4096; the first test observes the cells (0, 0, 0) and (15, 255, 4095). `block_cols`: row r lists 7 different block columns, the first of which is r.
All inputs are finite; a program needn't handle non-finite values. No bound on the sum of `fixed_mask` on one device may be relied on, other than what follows from the above.
Results may differ from a plain program's by a relative error of at most 0.0029.
Values may be sent and summed in bfloat16 or wider, within the bound.
No kernel may reach another device: no remote copies, remote signals or barrier semaphores. Data moves between devices by JAX's collectives and lax.ppermute only.
A program may use at most 64 MiB of HBM per device.

v0:
```python
import jax
import jax.numpy as jnp
from jax import lax
from jax.sharding import PartitionSpec as P


def extended(cells, sides, width):
    for axis, dim in sides:
        count = lax.axis_size(axis)
        ends = count - 1
        head = lax.slice_in_dim(cells, 0, width, axis=dim)
        tail = lax.slice_in_dim(cells, cells.shape[dim] - width, cells.shape[dim], axis=dim)
        cells = jnp.concatenate(
            [
                lax.ppermute(tail, axis, [(i, (i + 1) % count) for i in range(ends)]),
                cells,
                lax.ppermute(head, axis, [((i + 1) % count, i) for i in range(ends)]),
            ],
            axis=dim,
        )
    return cells


def shifted(padded):
    lead = [(0, 0)] * (padded.ndim - 3)
    deeper = jnp.pad(padded, lead + [(1, 1), (0, 0), (0, 0)])
    centre = deeper[..., 1:-1, 1:-1, 1:-1]
    beside_all = [
        deeper[..., 2:, 1:-1, 1:-1],
        deeper[..., :-2, 1:-1, 1:-1],
        deeper[..., 1:-1, 2:, 1:-1],
        deeper[..., 1:-1, :-2, 1:-1],
        deeper[..., 1:-1, 1:-1, 2:],
        deeper[..., 1:-1, 1:-1, :-2],
    ]
    return (centre, beside_all)


def face_weights(kappa_pad):
    centre, beside_all = shifted(kappa_pad)
    return [
        2.0 * centre * other / jnp.where(centre + other > 0.0, centre + other, 1.0)
        for other in beside_all
    ]


def advance(adjoint_pad, weights, keep, speed_x, speed_y, source):
    centre, beside_all = shifted(adjoint_pad)
    diffusion = weights[0] * (beside_all[0] - centre)
    for face in range(1, 6):
        diffusion = diffusion + weights[face] * (beside_all[face] - centre)
    slope_x = 0.5 * (beside_all[2] - beside_all[3])
    slope_y = 0.5 * (beside_all[4] - beside_all[5])
    updated = keep * (centre + diffusion + speed_x * slope_x + speed_y * slope_y + source)
    return (updated, diffusion, slope_x, slope_y)


def well_sources(wells, misfit_level, layers, rows_x, cols_y, margin):
    start_x = lax.axis_index("gx") * rows_x - margin
    start_y = lax.axis_index("gy") * cols_y - margin
    coord_z = jnp.arange(layers, dtype=jnp.int32)[:, None, None]
    coord_x = (start_x + jnp.arange(rows_x + 2 * margin, dtype=jnp.int32))[None, :, None]
    coord_y = (start_y + jnp.arange(cols_y + 2 * margin, dtype=jnp.int32))[None, None, :]
    well_z = wells[:, :, 0][:, :, None, None, None]
    well_x = wells[:, :, 1][:, :, None, None, None]
    well_y = wells[:, :, 2][:, :, None, None, None]
    matches = (coord_z == well_z) & (coord_x == well_x) & (coord_y == well_y)
    return jnp.sum(jnp.where(matches, misfit_level[:, :, None, None, None], 0.0), axis=1)


def shards(
    terminal,
    forward_temp,
    conductivity,
    velocity,
    fixed_mask,
    wells,
    misfit,
    head_gradient,
    blocks,
    block_cols,
):
    layers, rows_x, cols_y = conductivity.shape
    steps = forward_temp.shape[0]
    keep = 1.0 - fixed_mask.astype(jnp.float32)
    heat_sens = jnp.zeros((layers, rows_x, cols_y), jnp.float32)
    flow_x = jnp.zeros((layers, rows_x, cols_y), jnp.float32)
    flow_y = jnp.zeros((layers, rows_x, cols_y), jnp.float32)
    kappa_pad = extended(conductivity, (("gx", 1), ("gy", 2)), 1)
    weights = face_weights(kappa_pad)
    adjoint = terminal
    for level in reversed(range(steps)):
        padded = extended(adjoint, (("gx", 2), ("gy", 3)), 1)
        source = well_sources(wells, misfit[level], layers, rows_x, cols_y, 0)
        adjoint, diffusion, slope_x, slope_y = advance(
            padded, weights, keep, velocity[0], velocity[1], source
        )
        temper = forward_temp[level].astype(jnp.float32)
        heat_sens = heat_sens + jnp.sum(temper * diffusion, axis=0)
        flow_x = flow_x + jnp.sum(temper * slope_x, axis=0)
        flow_y = flow_y + jnp.sum(temper * slope_y, axis=0)
    summed = lax.psum_scatter(jnp.stack([flow_x, flow_y]), "sec", scatter_dimension=0, tiled=True)
    rounded = summed[0].astype(jnp.bfloat16)
    row_blocks, per_row, block_size, _ = blocks.shape
    piece = lax.all_gather(rounded, "gy", axis=2, tiled=True)
    count = piece.shape[2] // block_size
    split_rows = piece.reshape(layers, rows_x, count, block_size)
    block_ids = jnp.arange(count, dtype=jnp.int32)
    chosen = (block_cols[:, :, None] == block_ids[None, None, :]).astype(jnp.bfloat16)
    portion = jnp.einsum("bkq,zxqj->bkzxj", chosen, split_rows, preferred_element_type=jnp.float32)
    picked = portion.astype(jnp.bfloat16)
    head = jnp.einsum(
        "bkzxj,bkij->zxbi", picked, blocks, preferred_element_type=jnp.float32
    ).reshape(layers, rows_x, cols_y)
    partial_sens = heat_sens + head * head_gradient[0].astype(jnp.float32)
    sensitivity = lax.psum(partial_sens, "sec")
    return (head[None], sensitivity)


def solution(mesh):
    placed = (
        P("sec", None, "gx", "gy"),
        P(None, "sec", None, "gx", "gy"),
        P(None, "gx", "gy"),
        P(None, None, "gx", "gy"),
        P(None, "gx", "gy"),
        P("sec", None, None),
        P(None, "sec", None),
        P("sec", None, "gx", "gy"),
        P("gy", None, None, None),
        P("gy", None),
    )
    return jax.shard_map(
        shards,
        mesh=mesh,
        in_specs=placed,
        out_specs=(P("sec", None, "gx", "gy"), P(None, "gx", "gy")),
        check_vma=False,
    )
```

profile of v0, /device:TPU:1, one launch (start us, length us, event | category | flops | bytes accessed | tf_op | source)
XLA Modules:
  0.0 278.9 jit_solution(739867863807899032)
XLA Ops:
  8.3 4.9 %collective-permute-start.2 = (f32[16,1,256]{2,1,0:T(1,128)S(1)}, f32[16,1,256]{2,1,0:T(1,128)S(1)}, u32[]{:S(2)}, u32[]{:S(2)}) collective-permute-start(f32[16,1,256]{2,1,0:T(1,128)S(1)} %get-tuple-element.29), channel_id=1, source_target_pairs={{0,16},{16,32},{32,48},{48,64},{64,80},{80,96},{96,112},{112,128},... | collective-permute-start | bytes 49160 | tf_op jit(solution)/shard_map/ppermute | solution.py:15
  13.3 5.1 %collective-permute-start.3 = (f32[16,1,256]{2,1,0:T(1,128)S(1)}, f32[16,1,256]{2,1,0:T(1,128)S(1)}, u32[]{:S(2)}, u32[]{:S(2)}) collective-permute-start(f32[16,1,256]{2,1,0:T(1,128)S(1)} %get-tuple-element.30), channel_id=1, source_target_pairs={{16,0},{32,16},{48,32},{64,48},{80,64},{96,80},{112,96},{128,112},... | collective-permute-start | bytes 49160 | tf_op jit(solution)/shard_map/ppermute | solution.py:17
  19.5 1.9 collective-permute-start
  21.4 3.6 %collective-permute-start.1 = (f32[2,16,1,256]{3,2,1,0:T(1,128)S(1)}, f32[2,16,1,256]{3,2,1,0:T(1,128)S(1)}, u32[]{:S(2)}, u32[]{:S(2)}) collective-permute-start(f32[2,16,1,256]{3,2,1,0:T(1,128)S(1)} %get-tuple-element.20), channel_id=1, source_target_pairs={{0,16},{16,32},{32,48},{48,64},{64,80},{80,96},{96,112},{112,128},... | collective-permute-start | bytes 98312 | tf_op jit(solution)/shard_map/ppermute | solution.py:15
  27.5 1.4 collective-permute-start.4
  28.9 1.3 collective-permute-start.5
  31.1 1.5 collective-permute-done.4
  32.6 4.1 %collective-permute-done.5 = f32[16,18,1]{2,1,0:T(8,128)S(1)} collective-permute-done((f32[16,18,1]{2,1,0:T(8,128)S(1)}, f32[16,18,1]{2,1,0:T(8,128)S(1)}, u32[]{:S(2)}, u32[]{:S(2)}) %collective-permute-start.5) | collective-permute-done | bytes 1184 | tf_op jit(solution)/shard_map/ppermute | solution.py:17
  37.4 2.2 collective-permute-start.6
  41.5 6.3 %collective-permute-done.6 = f32[2,16,18,1]{3,2,1,0:T(8,128)S(1)} collective-permute-done((f32[2,16,18,1]{3,2,1,0:T(8,128)S(1)}, f32[2,16,18,1]{3,2,1,0:T(8,128)S(1)}, u32[]{:S(2)}, u32[]{:S(2)}) %collective-permute-start.6) | collective-permute-done | bytes 2336 | tf_op jit(solution)/shard_map/ppermute | solution.py:15
  47.8 3.8 %collective-permute-done.7 = f32[2,16,18,1]{3,2,1,0:T(8,128)S(1)} collective-permute-done((f32[2,16,18,1]{3,2,1,0:T(8,128)S(1)}, f32[2,16,18,1]{3,2,1,0:T(8,128)S(1)}, u32[]{:S(2)}, u32[]{:S(2)}) %collective-permute-start.7) | collective-permute-done | bytes 2336 | tf_op jit(solution)/shard_map/ppermute | solution.py:17
  53.5 3.3 %collective-permute-start.8 = (f32[2,16,1,256]{3,2,1,0:T(1,128)S(1)}, f32[2,16,1,256]{3,2,1,0:T(1,128)S(1)}, u32[]{:S(2)}, u32[]{:S(2)}) collective-permute-start(f32[2,16,1,256]{3,2,1,0:T(1,128)S(1)} %get-tuple-element.15), channel_id=1, source_target_pairs={{16,0},{32,16},{48,32},{64,48},{80,64},{96,80},{112,96},{128,112},... | collective-permute-start | bytes 98312 | tf_op jit(solution)/shard_map/ppermute | solution.py:17
  56.8 3.8 %collective-permute-start.9 = (f32[2,16,1,256]{3,2,1,0:T(1,128)S(1)}, f32[2,16,1,256]{3,2,1,0:T(1,128)S(1)}, u32[]{:S(2)}, u32[]{:S(2)}) collective-permute-start(f32[2,16,1,256]{3,2,1,0:T(1,128)S(1)} %get-tuple-element.16), channel_id=1, source_target_pairs={{0,16},{16,32},{32,48},{48,64},{64,80},{80,96},{96,112},{112,128},... | collective-permute-start | bytes 98312 | tf_op jit(solution)/shard_map/ppermute | solution.py:15
  63.2 5.1 %collective-permute-start.11 = (f32[2,16,18,1]{3,2,1,0:T(8,128)S(1)}, f32[2,16,18,1]{3,2,1,0:T(8,128)S(1)}, u32[]{:S(2)}, u32[]{:S(2)}) collective-permute-start(f32[2,16,18,1]{3,2,1,0:T(8,128)S(1)} %get-tuple-element.12), channel_id=1, source_target_pairs={{0,1},{1,2},{2,3},{3,4},{4,5},{5,6},{6,7},{7,8},{8,9},{9,10},{10,1... | collective-permute-start | bytes 6920 | tf_op jit(solution)/shard_map/ppermute | solution.py:15
  68.9 5.6 %collective-permute-done.10 = f32[2,16,18,1]{3,2,1,0:T(8,128)S(1)} collective-permute-done((f32[2,16,18,1]{3,2,1,0:T(8,128)S(1)}, f32[2,16,18,1]{3,2,1,0:T(8,128)S(1)}, u32[]{:S(2)}, u32[]{:S(2)}) %collective-permute-start.10) | collective-permute-done | bytes 2336 | tf_op jit(solution)/shard_map/ppermute | solution.py:17
  74.5 1.8 collective-permute-done.11
  76.2 1.3 fusion.7
  78.5 59.7 %reduce-scatter.2.cloned.1.call-done = f32[1,16,16,256]{3,2,1,0:T(8,128)} async-done(((f32[2,16,16,256]{3,2,1,0:T(8,128)}), f32[1,16,16,256]{3,2,1,0:T(8,128)}) %reduce-scatter.2.cloned.1.call-update) | async-done | bytes 262160 | tf_op jit(solution)/shard_map/reduce_scatter | solution.py:102
  138.3 1.6 convert_element_type.41
  141.0 1.7 fusion.9
  142.7 52.4 %all-gather.3.cloned.1.call-done = bf16[1,16,16,4096]{3,2,1,0:T(8,128)(2,1)} async-done(((bf16[1,16,16,256]{3,2,1,0:T(8,128)(2,1)}), bf16[1,16,16,4096]{3,2,1,0:T(8,128)(2,1)}) %all-gather.3.cloned.1.call-update) | async-done | bytes 2097168 | tf_op jit(solution)/shard_map/all_gather | solution.py:105
  195.1 2.1 copy.21
  200.7 70.0 %all-reduce.5.cloned.1.call-done = f32[16,16,256]{2,1,0:T(8,128)} async-done(((f32[16,16,256]{2,1,0:T(8,128)}), f32[16,16,256]{2,1,0:T(8,128)}) %all-reduce.5.cloned.1.call-update) | async-done | bytes 262160 | tf_op jit(solution)/shard_map/psum | solution.py:116
  270.7 1.7 copy.26
  (69 shorter events, 18.4 us)
Async XLA Ops:
  7.2 190.6 %copy-start = (bf16[2,7,128,128]{3,2,1,0:T(8,128)(2,1)S(1)}, bf16[2,7,128,128]{3,2,1,0:T(8,128)(2,1)}, u32[]{:S(2)}) copy-start(bf16[2,7,128,128]{3,2,1,0:T(8,128)(2,1)} %param.18) | copy-start | bytes 1376260
  7.2 20.1 %copy-start.2 = (f32[16,16,256]{2,1,0:T(8,128)S(1)}, f32[16,16,256]{2,1,0:T(8,128)}, u32[]{:S(2)}) copy-start(f32[16,16,256]{2,1,0:T(8,128)} %param.12) | copy-start | bytes 786436
  7.2 19.8 %copy-start.7 = (s32[16,16,256]{2,1,0:T(8,128)S(1)}, s32[16,16,256]{2,1,0:T(8,128)}, u32[]{:S(2)}) copy-start(s32[16,16,256]{2,1,0:T(8,128)} %param.14) | copy-start | bytes 786436
  7.2 20.1 %copy-start.10 = (f32[2,2,8]{2,1,0:T(2,128)S(1)}, f32[2,2,8]{2,1,0:T(2,128)}, u32[]{:S(2)}) copy-start(f32[2,2,8]{2,1,0:T(2,128)} %param.16) | copy-start | bytes 388
  7.2 131.1 %reduce-scatter.2.cloned.1.call-start = ((), (), s32[]{:S(2)}) async-start(), calls=%async_computation.1 | async-start | bytes 786432 | tf_op jit(solution)/shard_map/reduce_scatter | solution.py:102
  8.3 18.9 %collective-permute-start.2 = (f32[16,1,256]{2,1,0:T(1,128)S(1)}, f32[16,1,256]{2,1,0:T(1,128)S(1)}, u32[]{:S(2)}, u32[]{:S(2)}) collective-permute-start(f32[16,1,256]{2,1,0:T(1,128)S(1)} %get-tuple-element.29), channel_id=1, source_target_pairs={{0,16},{16,32},{32,48},{48,64},{64,80},{80,96},{96,112},{112,128},... | collective-permute-start | bytes 49160 | tf_op jit(solution)/shard_map/ppermute | solution.py:15
  13.3 14.0 %collective-permute-start.3 = (f32[16,1,256]{2,1,0:T(1,128)S(1)}, f32[16,1,256]{2,1,0:T(1,128)S(1)}, u32[]{:S(2)}, u32[]{:S(2)}) collective-permute-start(f32[16,1,256]{2,1,0:T(1,128)S(1)} %get-tuple-element.30), channel_id=1, source_target_pairs={{16,0},{32,16},{48,32},{64,48},{80,64},{96,80},{112,96},{128,112},... | collective-permute-start | bytes 49160 | tf_op jit(solution)/shard_map/ppermute | solution.py:17
  19.5 17.6 %collective-permute-start = (f32[2,16,1,256]{3,2,1,0:T(1,128)S(1)}, f32[2,16,1,256]{3,2,1,0:T(1,128)S(1)}, u32[]{:S(2)}, u32[]{:S(2)}) collective-permute-start(f32[2,16,1,256]{3,2,1,0:T(1,128)S(1)} %get-tuple-element.19), channel_id=1, source_target_pairs={{16,0},{32,16},{48,32},{64,48},{80,64},{96,80},{112,96},{128,112},... | collective-permute-start | bytes 98312 | tf_op jit(solution)/shard_map/ppermute | solution.py:17
  21.4 15.7 %collective-permute-start.1 = (f32[2,16,1,256]{3,2,1,0:T(1,128)S(1)}, f32[2,16,1,256]{3,2,1,0:T(1,128)S(1)}, u32[]{:S(2)}, u32[]{:S(2)}) collective-permute-start(f32[2,16,1,256]{3,2,1,0:T(1,128)S(1)} %get-tuple-element.20), channel_id=1, source_target_pairs={{0,16},{16,32},{32,48},{48,64},{64,80},{80,96},{96,112},{112,128},... | collective-permute-start | bytes 98312 | tf_op jit(solution)/shard_map/ppermute | solution.py:15
  27.4 9.7 %copy-start.1 = (f32[2,16,16,256]{3,2,1,0:T(8,128)S(1)}, f32[2,16,16,256]{3,2,1,0:T(8,128)}, u32[]{:S(2)}) copy-start(f32[2,16,16,256]{3,2,1,0:T(8,128)} %param.10) | copy-start | bytes 1572868
  27.5 5.1 %collective-permute-start.4 = (f32[16,18,1]{2,1,0:T(8,128)S(1)}, f32[16,18,1]{2,1,0:T(8,128)S(1)}, u32[]{:S(2)}, u32[]{:S(2)}) collective-permute-start(f32[16,18,1]{2,1,0:T(8,128)S(1)} %get-tuple-element.22), channel_id=1, source_target_pairs={{0,1},{1,2},{2,3},{3,4},{4,5},{5,6},{6,7},{7,8},{8,9},{9,10},{10,1... | collective-permute-start | bytes 3464 | tf_op jit(solution)/shard_map/ppermute | solution.py:15
  28.9 7.8 %collective-permute-start.5 = (f32[16,18,1]{2,1,0:T(8,128)S(1)}, f32[16,18,1]{2,1,0:T(8,128)S(1)}, u32[]{:S(2)}, u32[]{:S(2)}) collective-permute-start(f32[16,18,1]{2,1,0:T(8,128)S(1)} %get-tuple-element.21), channel_id=1, source_target_pairs={{1,0},{2,1},{3,2},{4,3},{5,4},{6,5},{7,6},{8,7},{9,8},{10,9},{11,1... | collective-permute-start | bytes 3464 | tf_op jit(solution)/shard_map/ppermute | solution.py:17
  37.4 10.4 %collective-permute-start.6 = (f32[2,16,18,1]{3,2,1,0:T(8,128)S(1)}, f32[2,16,18,1]{3,2,1,0:T(8,128)S(1)}, u32[]{:S(2)}, u32[]{:S(2)}) collective-permute-start(f32[2,16,18,1]{3,2,1,0:T(8,128)S(1)} %get-tuple-element.14), channel_id=1, source_target_pairs={{0,1},{1,2},{2,3},{3,4},{4,5},{5,6},{6,7},{7,8},{8,9},{9,10},{10,1... | collective-permute-start | bytes 6920 | tf_op jit(solution)/shard_map/ppermute | solution.py:15
  39.6 12.0 %collective-permute-start.7 = (f32[2,16,18,1]{3,2,1,0:T(8,128)S(1)}, f32[2,16,18,1]{3,2,1,0:T(8,128)S(1)}, u32[]{:S(2)}, u32[]{:S(2)}) collective-permute-start(f32[2,16,18,1]{3,2,1,0:T(8,128)S(1)} %get-tuple-element.13), channel_id=1, source_target_pairs={{1,0},{2,1},{3,2},{4,3},{5,4},{6,5},{7,6},{8,7},{9,8},{10,9},{11,1... | collective-permute-start | bytes 6920 | tf_op jit(solution)/shard_map/ppermute | solution.py:17
  53.5 7.1 %collective-permute-start.8 = (f32[2,16,1,256]{3,2,1,0:T(1,128)S(1)}, f32[2,16,1,256]{3,2,1,0:T(1,128)S(1)}, u32[]{:S(2)}, u32[]{:S(2)}) collective-permute-start(f32[2,16,1,256]{3,2,1,0:T(1,128)S(1)} %get-tuple-element.15), channel_id=1, source_target_pairs={{16,0},{32,16},{48,32},{64,48},{80,64},{96,80},{112,96},{128,112},... | collective-permute-start | bytes 98312 | tf_op jit(solution)/shard_map/ppermute | solution.py:17
  56.8 11.5 %copy-start.3 = (bf16[2,2,16,16,256]{4,3,2,1,0:T(8,128)(2,1)S(1)}, bf16[2,2,16,16,256]{4,3,2,1,0:T(8,128)(2,1)}, u32[]{:S(2)}) copy-start(bf16[2,2,16,16,256]{4,3,2,1,0:T(8,128)(2,1)} %param.11) | copy-start | bytes 1572868
  56.8 4.8 %collective-permute-start.9 = (f32[2,16,1,256]{3,2,1,0:T(1,128)S(1)}, f32[2,16,1,256]{3,2,1,0:T(1,128)S(1)}, u32[]{:S(2)}, u32[]{:S(2)}) collective-permute-start(f32[2,16,1,256]{3,2,1,0:T(1,128)S(1)} %get-tuple-element.16), channel_id=1, source_target_pairs={{0,16},{16,32},{32,48},{48,64},{64,80},{80,96},{96,112},{112,128},... | collective-permute-start | bytes 98312 | tf_op jit(solution)/shard_map/ppermute | solution.py:15
  61.9 12.6 %collective-permute-start.10 = (f32[2,16,18,1]{3,2,1,0:T(8,128)S(1)}, f32[2,16,18,1]{3,2,1,0:T(8,128)S(1)}, u32[]{:S(2)}, u32[]{:S(2)}) collective-permute-start(f32[2,16,18,1]{3,2,1,0:T(8,128)S(1)} %get-tuple-element.11), channel_id=1, source_target_pairs={{1,0},{2,1},{3,2},{4,3},{5,4},{6,5},{7,6},{8,7},{9,8},{10,9},{11,1... | collective-permute-start | bytes 6920 | tf_op jit(solution)/shard_map/ppermute | solution.py:17
  63.2 13.0 %collective-permute-start.11 = (f32[2,16,18,1]{3,2,1,0:T(8,128)S(1)}, f32[2,16,18,1]{3,2,1,0:T(8,128)S(1)}, u32[]{:S(2)}, u32[]{:S(2)}) collective-permute-start(f32[2,16,18,1]{3,2,1,0:T(8,128)S(1)} %get-tuple-element.12), channel_id=1, source_target_pairs={{0,1},{1,2},{2,3},{3,4},{4,5},{5,6},{6,7},{7,8},{8,9},{9,10},{10,1... | collective-permute-start | bytes 6920 | tf_op jit(solution)/shard_map/ppermute | solution.py:15
  78.5 116.6 %all-gather.3.cloned.1.call-start = ((), (), s32[]{:S(2)}) async-start(), calls=%async_computation.3 | async-start | bytes 2228224 | tf_op jit(solution)/shard_map/all_gather | solution.py:105
  139.9 130.8 %all-reduce.5.cloned.1.call-start = ((), (), s32[]{:S(2)}) async-start(), calls=%async_computation.2 | async-start | bytes 524288 | tf_op jit(solution)/shard_map/psum | solution.py:116
  140.0 1.0 copy-start.4
  195.1 2.1 copy-start.9
  197.8 1.0 copy-start.8
  (2 other events, 2.0 us)
Sparse Core Ops, SparseCore 0:
  78.6 59.6 reduce-scatter.1
  141.7 53.3 all-gather.2
  199.7 70.9 all-reduce.4
where the time goes:
time: 280 us; the launch traced here: 279 us
  waiting for transfers between devices  206 us (74%)
  starting transfers between devices  35.4 us (13%)
  between operations  14.1 us (5%)
  other arithmetic  12.9 us (5%)
  local copies, waits for them, and re-layouts  9.19 us (3%)
    psum x1, waiting for transfers between devices, shards(): sensitivity = lax.psum(partial_sens, 'sec')  70 us
    reduce_scatter x1, waiting for transfers between devices, shards(): lax.psum_scatter(jnp.stack([flow_x, flow_y]), 'sec', scatter_dimension=0,...  59.7 us
    all_gather x1, waiting for transfers between devices, shards(): piece = lax.all_gather(rounded, 'gy', axis=2, tiled=True)  52.4 us
    ppermute x6, starting transfers between devices, extended(): lax.ppermute(tail, axis, [(i, (i + 1) % count) for i in range(ends)])  21 us
    ppermute x6, starting transfers between devices, extended(): lax.ppermute(head, axis, [((i + 1) % count, i) for i in range(ends)])  14.3 us
    ppermute x6, waiting for transfers between devices, extended(): lax.ppermute(head, axis, [((i + 1) % count, i) for i in range(ends)])  13.5 us
    ppermute x6, waiting for transfers between devices, extended(): lax.ppermute(tail, axis, [(i, (i + 1) % count) for i in range(ends)])  10.6 us
  transfers between devices with their start and end apart: 15, of which 10 were waited for; matrix products, arithmetic and copies ran while one was open for 3% of the time, Pallas kernels for 0%

commit v1 on v0

--- a/solution.py
+++ b/solution.py
@@ -102,7 +102,9 @@
     summed = lax.psum_scatter(jnp.stack([flow_x, flow_y]), "sec", scatter_dimension=0, tiled=True)
     rounded = summed[0].astype(jnp.bfloat16)
     row_blocks, per_row, block_size, _ = blocks.shape
-    piece = lax.all_gather(rounded, "gy", axis=2, tiled=True)
+    piece = jnp.concatenate(
+        lax.all_to_all(jnp.stack(lax.axis_size("gy") * [rounded]), "gy", 0, 0), axis=2
+    )
     count = piece.shape[2] // block_size
     split_rows = piece.reshape(layers, rows_x, count, block_size)
     block_ids = jnp.arange(count, dtype=jnp.int32)

time: 280 us -> 254 us (0.907)
  waiting for transfers between devices: 206 us -> 169 us
  starting transfers between devices: 35.4 us -> 41.9 us
  local copies, waits for them, and re-layouts: 9.19 us -> 13.6 us
    all_gather x1 -> x0, waiting for transfers between devices: 52.4 us -> none  [shards(): piece = lax.all_gather(rounded, 'gy', axis=2, tiled=True)]
    all_to_all x0 -> x1, waiting for transfers between devices: none -> 24.3 us  [shards(): lax.all_to_all(jnp.stack(lax.axis_size('gy') * [rounded]), 'gy', 0, 0)]
    psum x1, waiting for transfers between devices: 70 us -> 60.4 us  [shards(): sensitivity = lax.psum(partial_sens, 'sec')]
    all_to_all x0 -> x1, starting transfers between devices: none -> 6.53 us  [shards(): lax.all_to_all(jnp.stack(lax.axis_size('gy') * [rounded]), 'gy', 0, 0)]
    another operation x0 -> x2, local copies, waits for them, and re-layouts: none -> 4.24 us  [the longest x1 2.69 us: shards(): split_rows = piece.reshape(layers, rows_x, count, block_size)]
  transfers between devices with their start and end apart: 15 -> 15, of which waited for: 10 -> 10; matrix products, arithmetic and copies ran while one was open for 3% -> 4% of each run, Pallas kernels for 0% -> 0%
where the time goes in v1:
time: 254 us; the launch traced here: 253 us
  waiting for transfers between devices  169 us (67%)
  starting transfers between devices  41.9 us (16%)
  between operations  14.7 us (6%)
  local copies, waits for them, and re-layouts  13.6 us (5%)
  other arithmetic  13.4 us (5%)
    psum x1, waiting for transfers between devices, shards(): sensitivity = lax.psum(partial_sens, 'sec')  60.4 us
    reduce_scatter x1, waiting for transfers between devices, shards(): lax.psum_scatter(jnp.stack([flow_x, flow_y]), 'sec', scatter_dimension=0,...  59.8 us
    all_to_all x1, waiting for transfers between devices, shards(): lax.all_to_all(jnp.stack(lax.axis_size('gy') * [rounded]), 'gy', 0, 0)  24.3 us
    ppermute x6, starting transfers between devices, extended(): lax.ppermute(tail, axis, [(i, (i + 1) % count) for i in range(ends)])  21 us
    ppermute x6, starting transfers between devices, extended(): lax.ppermute(head, axis, [((i + 1) % count, i) for i in range(ends)])  14.3 us
    ppermute x6, waiting for transfers between devices, extended(): lax.ppermute(head, axis, [((i + 1) % count, i) for i in range(ends)])  13.5 us
    ppermute x6, waiting for transfers between devices, extended(): lax.ppermute(tail, axis, [(i, (i + 1) % count) for i in range(ends)])  10.5 us
    all_to_all x1, starting transfers between devices, shards(): lax.all_to_all(jnp.stack(lax.axis_size('gy') * [rounded]), 'gy', 0, 0)  6.53 us
  transfers between devices with their start and end apart: 15, of which 10 were waited for; matrix products, arithmetic and copies ran while one was open for 4% of the time, Pallas kernels for 0%

profile of v1, /device:TPU:1, one launch (start us, length us, event | category | flops | bytes accessed | tf_op | source)
XLA Modules:
  0.0 253.2 jit_solution(18214689588705697450)
XLA Ops:
  8.3 4.9 %collective-permute-start.2 = (f32[16,1,256]{2,1,0:T(1,128)S(1)}, f32[16,1,256]{2,1,0:T(1,128)S(1)}, u32[]{:S(2)}, u32[]{:S(2)}) collective-permute-start(f32[16,1,256]{2,1,0:T(1,128)S(1)} %get-tuple-element.29), channel_id=1, source_target_pairs={{0,16},{16,32},{32,48},{48,64},{64,80},{80,96},{96,112},{112,128},... | collective-permute-start | bytes 49160 | tf_op jit(solution)/shard_map/ppermute | solution.py:15
  13.3 5.1 %collective-permute-start.3 = (f32[16,1,256]{2,1,0:T(1,128)S(1)}, f32[16,1,256]{2,1,0:T(1,128)S(1)}, u32[]{:S(2)}, u32[]{:S(2)}) collective-permute-start(f32[16,1,256]{2,1,0:T(1,128)S(1)} %get-tuple-element.30), channel_id=1, source_target_pairs={{16,0},{32,16},{48,32},{64,48},{80,64},{96,80},{112,96},{128,112},... | collective-permute-start | bytes 49160 | tf_op jit(solution)/shard_map/ppermute | solution.py:17
  19.5 1.9 collective-permute-start
  21.4 3.6 %collective-permute-start.1 = (f32[2,16,1,256]{3,2,1,0:T(1,128)S(1)}, f32[2,16,1,256]{3,2,1,0:T(1,128)S(1)}, u32[]{:S(2)}, u32[]{:S(2)}) collective-permute-start(f32[2,16,1,256]{3,2,1,0:T(1,128)S(1)} %get-tuple-element.20), channel_id=1, source_target_pairs={{0,16},{16,32},{32,48},{48,64},{64,80},{80,96},{96,112},{112,128},... | collective-permute-start | bytes 98312 | tf_op jit(solution)/shard_map/ppermute | solution.py:15
  31.1 1.5 collective-permute-done.4
  32.6 4.1 %collective-permute-done.5 = f32[16,18,1]{2,1,0:T(8,128)S(1)} collective-permute-done((f32[16,18,1]{2,1,0:T(8,128)S(1)}, f32[16,18,1]{2,1,0:T(8,128)S(1)}, u32[]{:S(2)}, u32[]{:S(2)}) %collective-permute-start.5) | collective-permute-done | bytes 1184 | tf_op jit(solution)/shard_map/ppermute | solution.py:17
  37.4 2.2 collective-permute-start.6
  41.5 6.3 %collective-permute-done.6 = f32[2,16,18,1]{3,2,1,0:T(8,128)S(1)} collective-permute-done((f32[2,16,18,1]{3,2,1,0:T(8,128)S(1)}, f32[2,16,18,1]{3,2,1,0:T(8,128)S(1)}, u32[]{:S(2)}, u32[]{:S(2)}) %collective-permute-start.6) | collective-permute-done | bytes 2336 | tf_op jit(solution)/shard_map/ppermute | solution.py:15
  47.8 3.8 %collective-permute-done.7 = f32[2,16,18,1]{3,2,1,0:T(8,128)S(1)} collective-permute-done((f32[2,16,18,1]{3,2,1,0:T(8,128)S(1)}, f32[2,16,18,1]{3,2,1,0:T(8,128)S(1)}, u32[]{:S(2)}, u32[]{:S(2)}) %collective-permute-start.7) | collective-permute-done | bytes 2336 | tf_op jit(solution)/shard_map/ppermute | solution.py:17
  53.5 3.3 %collective-permute-start.8 = (f32[2,16,1,256]{3,2,1,0:T(1,128)S(1)}, f32[2,16,1,256]{3,2,1,0:T(1,128)S(1)}, u32[]{:S(2)}, u32[]{:S(2)}) collective-permute-start(f32[2,16,1,256]{3,2,1,0:T(1,128)S(1)} %get-tuple-element.15), channel_id=1, source_target_pairs={{16,0},{32,16},{48,32},{64,48},{80,64},{96,80},{112,96},{128,112},... | collective-permute-start | bytes 98312 | tf_op jit(solution)/shard_map/ppermute | solution.py:17
  56.8 3.8 %collective-permute-start.9 = (f32[2,16,1,256]{3,2,1,0:T(1,128)S(1)}, f32[2,16,1,256]{3,2,1,0:T(1,128)S(1)}, u32[]{:S(2)}, u32[]{:S(2)}) collective-permute-start(f32[2,16,1,256]{3,2,1,0:T(1,128)S(1)} %get-tuple-element.16), channel_id=1, source_target_pairs={{0,16},{16,32},{32,48},{48,64},{64,80},{80,96},{96,112},{112,128},... | collective-permute-start | bytes 98312 | tf_op jit(solution)/shard_map/ppermute | solution.py:15
  63.2 5.1 %collective-permute-start.11 = (f32[2,16,18,1]{3,2,1,0:T(8,128)S(1)}, f32[2,16,18,1]{3,2,1,0:T(8,128)S(1)}, u32[]{:S(2)}, u32[]{:S(2)}) collective-permute-start(f32[2,16,18,1]{3,2,1,0:T(8,128)S(1)} %get-tuple-element.12), channel_id=1, source_target_pairs={{0,1},{1,2},{2,3},{3,4},{4,5},{5,6},{6,7},{7,8},{8,9},{9,10},{10,1... | collective-permute-start | bytes 6920 | tf_op jit(solution)/shard_map/ppermute | solution.py:15
  68.9 5.6 %collective-permute-done.10 = f32[2,16,18,1]{3,2,1,0:T(8,128)S(1)} collective-permute-done((f32[2,16,18,1]{3,2,1,0:T(8,128)S(1)}, f32[2,16,18,1]{3,2,1,0:T(8,128)S(1)}, u32[]{:S(2)}, u32[]{:S(2)}) %collective-permute-start.10) | collective-permute-done | bytes 2336 | tf_op jit(solution)/shard_map/ppermute | solution.py:17
  74.5 1.8 collective-permute-done.11
  78.5 59.8 %reduce-scatter.2.cloned.1.call-done = f32[1,16,16,256]{3,2,1,0:T(8,128)} async-done(((f32[2,16,16,256]{3,2,1,0:T(8,128)}), f32[1,16,16,256]{3,2,1,0:T(8,128)}) %reduce-scatter.2.cloned.1.call-update) | async-done | bytes 262160 | tf_op jit(solution)/shard_map/reduce_scatter | solution.py:102
  139.3 1.6 stack.8
  140.8 6.5 %all-to-all-start = ((bf16[16,16,16,256]{3,2,1,0:T(8,128)(2,1)}), bf16[16,16,16,256]{3,2,1,0:T(8,128)(2,1)S(1)}, u32[]{:S(2)}, u32[]{:S(2)}) async-start(bf16[16,16,16,256]{3,2,1,0:T(8,128)(2,1)} %stack.8), calls=%async_computation.1 | async-start | bytes 4194304 | tf_op jit(solution)/shard_map/all_to_all | solution.py:106
  147.5 1.9 select_maximum_fusion
  149.5 1.7 fusion.9
  151.2 24.3 %all-to-all-done = bf16[16,16,16,256]{3,2,1,0:T(8,128)(2,1)S(1)} async-done(((bf16[16,16,16,256]{3,2,1,0:T(8,128)(2,1)}), bf16[16,16,16,256]{3,2,1,0:T(8,128)(2,1)S(1)}, u32[]{:S(2)}, u32[]{:S(2)}) %all-to-all-start) | async-done | bytes 2097184 | tf_op jit(solution)/shard_map/all_to_all | solution.py:106
  175.5 2.5 copy.18
  178.0 2.7 %reshape.96 = bf16[16,16,32,128,1]{3,2,1,0,4:T(8,128)(2,1)S(1)} reshape(bf16[16,16,16,256]{3,2,1,0:T(8,128)(2,1)} %copy.18) | data formatting | bytes 4194304 | tf_op jit(solution)/shard_map/reshape;reshape | solution.py:109
  184.2 60.4 %all-reduce.5.cloned.1.call-done = f32[16,16,256]{2,1,0:T(8,128)} async-done(((f32[16,16,256]{2,1,0:T(8,128)}), f32[16,16,256]{2,1,0:T(8,128)}) %all-reduce.5.cloned.1.call-update) | async-done | bytes 262160 | tf_op jit(solution)/shard_map/psum | solution.py:118
  244.7 1.7 copy.30
  (98 shorter events, 22.4 us)
Async XLA Ops:
  7.2 174.1 %copy-start = (bf16[2,7,128,128]{3,2,1,0:T(8,128)(2,1)S(1)}, bf16[2,7,128,128]{3,2,1,0:T(8,128)(2,1)}, u32[]{:S(2)}) copy-start(bf16[2,7,128,128]{3,2,1,0:T(8,128)(2,1)} %param.18) | copy-start | bytes 1376260
  7.2 20.1 %copy-start.4 = (f32[16,16,256]{2,1,0:T(8,128)S(1)}, f32[16,16,256]{2,1,0:T(8,128)}, u32[]{:S(2)}) copy-start(f32[16,16,256]{2,1,0:T(8,128)} %param.12) | copy-start | bytes 786436
  7.2 19.8 %copy-start.21 = (s32[16,16,256]{2,1,0:T(8,128)S(1)}, s32[16,16,256]{2,1,0:T(8,128)}, u32[]{:S(2)}) copy-start(s32[16,16,256]{2,1,0:T(8,128)} %param.14) | copy-start | bytes 786436
  7.2 20.1 %copy-start.24 = (f32[2,2,8]{2,1,0:T(2,128)S(1)}, f32[2,2,8]{2,1,0:T(2,128)}, u32[]{:S(2)}) copy-start(f32[2,2,8]{2,1,0:T(2,128)} %param.16) | copy-start | bytes 388
  7.2 131.1 %reduce-scatter.2.cloned.1.call-start = ((), (), s32[]{:S(2)}) async-start(), calls=%async_computation.2 | async-start | bytes 786432 | tf_op jit(solution)/shard_map/reduce_scatter | solution.py:102
  8.3 18.9 %collective-permute-start.2 = (f32[16,1,256]{2,1,0:T(1,128)S(1)}, f32[16,1,256]{2,1,0:T(1,128)S(1)}, u32[]{:S(2)}, u32[]{:S(2)}) collective-permute-start(f32[16,1,256]{2,1,0:T(1,128)S(1)} %get-tuple-element.29), channel_id=1, source_target_pairs={{0,16},{16,32},{32,48},{48,64},{64,80},{80,96},{96,112},{112,128},... | collective-permute-start | bytes 49160 | tf_op jit(solution)/shard_map/ppermute | solution.py:15
  13.3 14.0 %collective-permute-start.3 = (f32[16,1,256]{2,1,0:T(1,128)S(1)}, f32[16,1,256]{2,1,0:T(1,128)S(1)}, u32[]{:S(2)}, u32[]{:S(2)}) collective-permute-start(f32[16,1,256]{2,1,0:T(1,128)S(1)} %get-tuple-element.30), channel_id=1, source_target_pairs={{16,0},{32,16},{48,32},{64,48},{80,64},{96,80},{112,96},{128,112},... | collective-permute-start | bytes 49160 | tf_op jit(solution)/shard_map/ppermute | solution.py:17
  19.5 17.6 %collective-permute-start = (f32[2,16,1,256]{3,2,1,0:T(1,128)S(1)}, f32[2,16,1,256]{3,2,1,0:T(1,128)S(1)}, u32[]{:S(2)}, u32[]{:S(2)}) collective-permute-start(f32[2,16,1,256]{3,2,1,0:T(1,128)S(1)} %get-tuple-element.19), channel_id=1, source_target_pairs={{16,0},{32,16},{48,32},{64,48},{80,64},{96,80},{112,96},{128,112},... | collective-permute-start | bytes 98312 | tf_op jit(solution)/shard_map/ppermute | solution.py:17
  21.4 15.7 %collective-permute-start.1 = (f32[2,16,1,256]{3,2,1,0:T(1,128)S(1)}, f32[2,16,1,256]{3,2,1,0:T(1,128)S(1)}, u32[]{:S(2)}, u32[]{:S(2)}) collective-permute-start(f32[2,16,1,256]{3,2,1,0:T(1,128)S(1)} %get-tuple-element.20), channel_id=1, source_target_pairs={{0,16},{16,32},{32,48},{48,64},{64,80},{80,96},{96,112},{112,128},... | collective-permute-start | bytes 98312 | tf_op jit(solution)/shard_map/ppermute | solution.py:15
  27.5 5.1 %collective-permute-start.4 = (f32[16,18,1]{2,1,0:T(8,128)S(1)}, f32[16,18,1]{2,1,0:T(8,128)S(1)}, u32[]{:S(2)}, u32[]{:S(2)}) collective-permute-start(f32[16,18,1]{2,1,0:T(8,128)S(1)} %get-tuple-element.22), channel_id=1, source_target_pairs={{0,1},{1,2},{2,3},{3,4},{4,5},{5,6},{6,7},{7,8},{8,9},{9,10},{10,1... | collective-permute-start | bytes 3464 | tf_op jit(solution)/shard_map/ppermute | solution.py:15
  28.9 7.8 %collective-permute-start.5 = (f32[16,18,1]{2,1,0:T(8,128)S(1)}, f32[16,18,1]{2,1,0:T(8,128)S(1)}, u32[]{:S(2)}, u32[]{:S(2)}) collective-permute-start(f32[16,18,1]{2,1,0:T(8,128)S(1)} %get-tuple-element.21), channel_id=1, source_target_pairs={{1,0},{2,1},{3,2},{4,3},{5,4},{6,5},{7,6},{8,7},{9,8},{10,9},{11,1... | collective-permute-start | bytes 3464 | tf_op jit(solution)/shard_map/ppermute | solution.py:17
  37.4 10.4 %collective-permute-start.6 = (f32[2,16,18,1]{3,2,1,0:T(8,128)S(1)}, f32[2,16,18,1]{3,2,1,0:T(8,128)S(1)}, u32[]{:S(2)}, u32[]{:S(2)}) collective-permute-start(f32[2,16,18,1]{3,2,1,0:T(8,128)S(1)} %get-tuple-element.14), channel_id=1, source_target_pairs={{0,1},{1,2},{2,3},{3,4},{4,5},{5,6},{6,7},{7,8},{8,9},{9,10},{10,1... | collective-permute-start | bytes 6920 | tf_op jit(solution)/shard_map/ppermute | solution.py:15
  39.6 12.0 %collective-permute-start.7 = (f32[2,16,18,1]{3,2,1,0:T(8,128)S(1)}, f32[2,16,18,1]{3,2,1,0:T(8,128)S(1)}, u32[]{:S(2)}, u32[]{:S(2)}) collective-permute-start(f32[2,16,18,1]{3,2,1,0:T(8,128)S(1)} %get-tuple-element.13), channel_id=1, source_target_pairs={{1,0},{2,1},{3,2},{4,3},{5,4},{6,5},{7,6},{8,7},{9,8},{10,9},{11,1... | collective-permute-start | bytes 6920 | tf_op jit(solution)/shard_map/ppermute | solution.py:17
  41.5 10.9 %copy-start.5 = (f32[16,16,256]{2,1,0:T(8,128)}, f32[16,16,256]{2,1,0:T(8,128)S(1)}, u32[]{:S(2)}) copy-start(f32[16,16,256]{2,1,0:T(8,128)S(1)} %get-tuple-element.23) | copy-start | bytes 786436
  41.5 10.9 %copy-start.7 = (f32[16,16,256]{2,1,0:T(8,128)}, f32[16,16,256]{2,1,0:T(8,128)S(1)}, u32[]{:S(2)}) copy-start(f32[16,16,256]{2,1,0:T(8,128)S(1)} %get-tuple-element.24) | copy-start | bytes 786436
  41.5 10.9 %copy-start.9 = (f32[16,16,256]{2,1,0:T(8,128)}, f32[16,16,256]{2,1,0:T(8,128)S(1)}, u32[]{:S(2)}) copy-start(f32[16,16,256]{2,1,0:T(8,128)S(1)} %get-tuple-element.25) | copy-start | bytes 786436
  41.5 10.9 %copy-start.11 = (f32[16,16,256]{2,1,0:T(8,128)}, f32[16,16,256]{2,1,0:T(8,128)S(1)}, u32[]{:S(2)}) copy-start(f32[16,16,256]{2,1,0:T(8,128)S(1)} %get-tuple-element.26) | copy-start | bytes 786436
  53.5 7.1 %collective-permute-start.8 = (f32[2,16,1,256]{3,2,1,0:T(1,128)S(1)}, f32[2,16,1,256]{3,2,1,0:T(1,128)S(1)}, u32[]{:S(2)}, u32[]{:S(2)}) collective-permute-start(f32[2,16,1,256]{3,2,1,0:T(1,128)S(1)} %get-tuple-element.15), channel_id=1, source_target_pairs={{16,0},{32,16},{48,32},{64,48},{80,64},{96,80},{112,96},{128,112},... | collective-permute-start | bytes 98312 | tf_op jit(solution)/shard_map/ppermute | solution.py:17
  56.8 11.5 %copy-start.17 = (bf16[2,2,16,16,256]{4,3,2,1,0:T(8,128)(2,1)S(1)}, bf16[2,2,16,16,256]{4,3,2,1,0:T(8,128)(2,1)}, u32[]{:S(2)}) copy-start(bf16[2,2,16,16,256]{4,3,2,1,0:T(8,128)(2,1)} %param.11) | copy-start | bytes 1572868
  56.8 4.8 %collective-permute-start.9 = (f32[2,16,1,256]{3,2,1,0:T(1,128)S(1)}, f32[2,16,1,256]{3,2,1,0:T(1,128)S(1)}, u32[]{:S(2)}, u32[]{:S(2)}) collective-permute-start(f32[2,16,1,256]{3,2,1,0:T(1,128)S(1)} %get-tuple-element.16), channel_id=1, source_target_pairs={{0,16},{16,32},{32,48},{48,64},{64,80},{80,96},{96,112},{112,128},... | collective-permute-start | bytes 98312 | tf_op jit(solution)/shard_map/ppermute | solution.py:15
  61.9 12.6 %collective-permute-start.10 = (f32[2,16,18,1]{3,2,1,0:T(8,128)S(1)}, f32[2,16,18,1]{3,2,1,0:T(8,128)S(1)}, u32[]{:S(2)}, u32[]{:S(2)}) collective-permute-start(f32[2,16,18,1]{3,2,1,0:T(8,128)S(1)} %get-tuple-element.11), channel_id=1, source_target_pairs={{1,0},{2,1},{3,2},{4,3},{5,4},{6,5},{7,6},{8,7},{9,8},{10,9},{11,1... | collective-permute-start | bytes 6920 | tf_op jit(solution)/shard_map/ppermute | solution.py:17
  63.2 13.0 %collective-permute-start.11 = (f32[2,16,18,1]{3,2,1,0:T(8,128)S(1)}, f32[2,16,18,1]{3,2,1,0:T(8,128)S(1)}, u32[]{:S(2)}, u32[]{:S(2)}) collective-permute-start(f32[2,16,18,1]{3,2,1,0:T(8,128)S(1)} %get-tuple-element.12), channel_id=1, source_target_pairs={{0,1},{1,2},{2,3},{3,4},{4,5},{5,6},{6,7},{7,8},{8,9},{9,10},{10,1... | collective-permute-start | bytes 6920 | tf_op jit(solution)/shard_map/ppermute | solution.py:15
  140.8 34.7 %all-to-all-start = ((bf16[16,16,16,256]{3,2,1,0:T(8,128)(2,1)}), bf16[16,16,16,256]{3,2,1,0:T(8,128)(2,1)S(1)}, u32[]{:S(2)}, u32[]{:S(2)}) async-start(bf16[16,16,16,256]{3,2,1,0:T(8,128)(2,1)} %stack.8), calls=%async_computation.1 | async-start | bytes 4194304 | tf_op jit(solution)/shard_map/all_to_all | solution.py:106
  147.4 97.3 %all-reduce.5.cloned.1.call-start = ((), (), s32[]{:S(2)}) async-start(), calls=%async_computation.3 | async-start | bytes 524288 | tf_op jit(solution)/shard_map/psum | solution.py:118
  (16 other events, 54.2 us)
Sparse Core Ops, SparseCore 0:
  78.7 59.6 reduce-scatter.1
  183.2 61.3 all-reduce.4
